TPU v7x, 32 devices: a whole 2x2x4 slice. The times are simulated.
32 devices in a mesh: blk: 16 (over z, y, x), col: 2 (over core).
Axes of the slice: x: 2, y: 2, z: 4, core: 2. Of those that a mesh axis runs over, the one named last changes fastest.
Arguments:
- trial: bfloat16 [32768, 128], P(('blk', 'col')), may hold values from -6 to 6
- omega: float32 [32768], P(('blk', 'col')), may hold values from 0.5 to 6
- table: bfloat16 [64, 128, 128], replicated, may hold values from -0.0625 to 0.0625
- block_type: int32 [256, 72], P(('blk', 'col')), may hold values from 0 to 63
- cycle_offset: int32 [256, 72], P(('blk', 'col')), may hold values from -4 to 4
- source_block: int32 [256, 72], P(('blk', 'col')), may hold values from 0 to 7
Outputs:
- sigma: bfloat16 [32768, 128], P(('blk', 'col'))
- projected: float32 [128, 128], replicated
- basis: float32 [32768, 128], P(('blk', 'col'))
All inputs are finite; a program needn't handle non-finite values.
Results may differ from a plain program's by a relative error of at most 0.006.
Values may be sent and summed in bfloat16 or wider, within the bound.
A program may use at most 64 MiB of HBM per device.

v0:
```python
import jax
import jax.numpy as jnp
from jax import lax
from jax.sharding import PartitionSpec as P

REACH = 4


def from_behind(value, axis, steps):
    count = lax.axis_size(axis)
    pairs = [(source, (source + steps) % count) for source in range(count)]
    return lax.ppermute(value, axis, pairs)


def on_device(trial, omega, table, block_type, cycle_offset, source_block):
    row_count = trial.shape[0]
    vec_count = trial.shape[1]
    pair_block = table.shape[1]
    blocks = row_count // pair_block
    own_slab = trial.reshape(blocks, pair_block, vec_count)
    slabs = {0: own_slab}
    offsets = [offset for offset in range(0 - REACH, REACH + 1) if offset != 0]
    for offset in offsets:
        slabs[offset] = from_behind(own_slab, "blk", 0 - offset)
    stacked = jnp.stack([slabs[offset] for offset in range(0 - REACH, REACH + 1)])
    stacked = stacked.reshape((2 * REACH + 1) * blocks, pair_block, vec_count)
    tile_index = (cycle_offset + REACH) * blocks + source_block
    energy = omega.reshape(blocks, pair_block)

    def one_block(operands):
        kinds, chosen, energy_row, own_rows = operands
        sources = stacked[chosen]
        coeffs = table[kinds]
        coupled = jnp.einsum("jab,jbk->ak", coeffs, sources, preferred_element_type=jnp.float32)
        return (coupled + energy_row[:, None] * own_rows.astype(jnp.float32)).astype(jnp.bfloat16)

    sigma = lax.map(one_block, (block_type, tile_index, energy, own_slab)).reshape(
        row_count, vec_count
    )
    highest = lax.Precision.HIGHEST
    sigma_full = sigma.astype(jnp.float32)
    trial_full = trial.astype(jnp.float32)
    total = row_count * lax.axis_size("blk") * lax.axis_size("col")
    projected = (
        lax.psum(jnp.dot(trial_full.T, sigma_full, precision=highest), ("blk", "col")) / total
    )
    residual = sigma_full - jnp.dot(trial_full, projected, precision=highest)
    gram = lax.psum(jnp.dot(residual.T, residual, precision=highest), ("blk", "col")) / total
    lower = jnp.linalg.cholesky(gram)
    inverse = jax.scipy.linalg.solve_triangular(
        lower, jnp.eye(vec_count, dtype=jnp.float32), lower=True
    )
    basis = jnp.dot(residual, inverse.T, precision=highest)
    return (sigma, projected, basis)


def solution(mesh):
    placed = (
        P(("blk", "col"), None),
        P(("blk", "col")),
        P(),
        P(("blk", "col"), None),
        P(("blk", "col"), None),
        P(("blk", "col"), None),
    )
    return jax.shard_map(
        on_device,
        mesh=mesh,
        in_specs=placed,
        out_specs=(P(("blk", "col"), None), P(), P(("blk", "col"), None)),
        check_vma=False,
    )
```

profile of v0, /device:TPU:1, one launch (start us, length us, event | category | flops | bytes accessed | tf_op | source)
XLA Modules:
  0.0 412.3 jit_solution(719922442792126760)
XLA Ops:
  7.2 2.2 collective-permute-start
  9.4 2.2 collective-permute-start.1
  11.6 1.2 collective-permute-start.2
  13.1 4.7 %collective-permute-start.4 = (bf16[8,128,128]{2,1,0:T(8,128)(2,1)}, bf16[8,128,128]{2,1,0:T(8,128)(2,1)S(1)}, u32[]{:S(2)}, u32[]{:S(2)}) collective-permute-start(bf16[8,128,128]{2,1,0:T(8,128)(2,1)} %bitcast.101), channel_id=1, source_target_pairs={{0,30},{2,0},{4,2},{6,4},{8,6},{10,8},{12,10},{14,12},{16,14},{18,... | collective-permute-start | bytes 786440 | tf_op jit(solution)/shard_map/ppermute | solution.py:12
  18.6 1.2 collective-permute-start.5
  19.8 4.2 %collective-permute-done.1 = bf16[8,128,128]{2,1,0:T(8,128)(2,1)S(1)} collective-permute-done((bf16[8,128,128]{2,1,0:T(8,128)(2,1)}, bf16[8,128,128]{2,1,0:T(8,128)(2,1)S(1)}, u32[]{:S(2)}, u32[]{:S(2)}) %collective-permute-start.1) | collective-permute-done | bytes 262176 | tf_op jit(solution)/shard_map/ppermute | solution.py:12
  24.0 2.3 collective-permute-start.6
  26.4 4.2 %collective-permute-done.2 = bf16[8,128,128]{2,1,0:T(8,128)(2,1)S(1)} collective-permute-done((bf16[8,128,128]{2,1,0:T(8,128)(2,1)}, bf16[8,128,128]{2,1,0:T(8,128)(2,1)S(1)}, u32[]{:S(2)}, u32[]{:S(2)}) %collective-permute-start.2) | collective-permute-done | bytes 262176 | tf_op jit(solution)/shard_map/ppermute | solution.py:12
  30.5 1.5 collective-permute-start.7
  32.1 6.1 %collective-permute-done.3 = bf16[8,128,128]{2,1,0:T(8,128)(2,1)S(1)} collective-permute-done((bf16[8,128,128]{2,1,0:T(8,128)(2,1)}, bf16[8,128,128]{2,1,0:T(8,128)(2,1)S(1)}, u32[]{:S(2)}, u32[]{:S(2)}) %collective-permute-start.3) | collective-permute-done | bytes 262176 | tf_op jit(solution)/shard_map/ppermute | solution.py:12
  38.2 1.0 constant_dynamic-update-slice_fusion
  39.3 1.0 collective-permute-done.6
  40.5 1.4 copy-done
  41.9 84.5 %while.10 = (s32[]{:T(128)}, bf16[8,128,128]{2,1,0:T(8,128)(2,1)S(1)}, s32[8,72]{1,0:T(8,128)}, bf16[64,128,128]{2,1,0:T(8,128)(2,1)}, s32[8,72]{1,0:T(8,128)S(1...) while((s32[]{:T(128)}, ...), condition=%wide.region_1.2_spmd, body=%wide.region_0.1_spmd.sunk | while | flops 302057920 | bytes 14233449 | solution.py:37
  42.6 2.6 gather_fusion
  45.2 4.1 gather_fusion.1
  50.0 2.4 fusion.34
  53.1 2.6 gather_fusion
  55.8 4.1 gather_fusion.1
  60.5 2.4 fusion.34
  63.7 2.6 gather_fusion
  66.3 4.1 gather_fusion.1
  71.1 2.4 fusion.34
  74.3 2.6 gather_fusion
  76.9 4.1 gather_fusion.1
  81.7 2.4 fusion.34
  84.8 2.6 gather_fusion
  87.5 4.1 gather_fusion.1
  92.2 2.4 fusion.34
  95.4 2.6 gather_fusion
  98.0 4.1 gather_fusion.1
  102.8 2.4 fusion.34
  106.0 2.6 gather_fusion
  108.6 4.1 gather_fusion.1
  113.4 2.4 fusion.34
  116.6 2.6 gather_fusion
  119.2 4.1 gather_fusion.1
  124.0 2.4 fusion.34
  126.4 0.9 convolution_bitcast_fusion.2
  127.5 126.7 %all-reduce.3.cloned.1.call-done = f32[128,128]{0,1:T(8,128)} async-done(((f32[128,128]{0,1:T(8,128)}), f32[128,128]{0,1:T(8,128)}) %all-reduce.3.cloned.1.call-update) | async-done | bytes 65552 | tf_op jit(solution)/shard_map/psum | solution.py:45
  254.2 1.2 fusion.9
  255.5 1.2 fusion.14
  256.7 0.8 broadcast_multiply_fusion.1
  258.3 120.5 %all-reduce.5.cloned.1.call-done = f32[128,128]{0,1:T(8,128)} async-done(((f32[128,128]{0,1:T(8,128)}), f32[128,128]{0,1:T(8,128)}) %all-reduce.5.cloned.1.call-update) | async-done | bytes 65552 | tf_op jit(solution)/shard_map/psum | solution.py:48
  379.7 0.9 fusion.13
  380.6 11.7 %cholesky.17 = f32[128,128]{1,0:T(8,128)S(1)} custom-call(f32[128,128]{1,0:T(8,128)S(1)} %fusion.13), custom_call_target="Cholesky" | custom-call | tf_op jit(solution)/shard_map/jit(cholesky)/cholesky | solution.py:49
  393.6 9.8 %custom-call.7 = f32[1,128,128]{1,2,0:T(8,128)S(1)} custom-call(f32[1,128,128]{2,1,0:T(8,128)S(1)} %fusion.10), custom_call_target="InvertDiagBlocksLowerTriangular" | custom-call | tf_op jit(solution)/shard_map/jit(_solve_triangular)/triangular_solve | solution.py:50
  403.7 1.8 fusion.15
  (64 shorter events, 16.0 us)
Async XLA Ops:
  7.2 247.1 %all-reduce.3.cloned.1.call-start = ((), (), s32[]{:S(2)}) async-start(), calls=%async_computation | async-start | bytes 131072 | tf_op jit(solution)/shard_map/psum | solution.py:45
  7.2 11.4 %collective-permute-start = (bf16[8,128,128]{2,1,0:T(8,128)(2,1)}, bf16[8,128,128]{2,1,0:T(8,128)(2,1)S(1)}, u32[]{:S(2)}, u32[]{:S(2)}) collective-permute-start(bf16[8,128,128]{2,1,0:T(8,128)(2,1)} %bitcast.97), channel_id=1, source_target_pairs={{0,8},{2,10},{4,12},{6,14},{8,16},{10,18},{12,20},{14,22},{16,24},... | collective-permute-start | bytes 786440 | tf_op jit(solution)/shard_map/ppermute | solution.py:12
  9.4 14.6 %collective-permute-start.1 = (bf16[8,128,128]{2,1,0:T(8,128)(2,1)}, bf16[8,128,128]{2,1,0:T(8,128)(2,1)S(1)}, u32[]{:S(2)}, u32[]{:S(2)}) collective-permute-start(bf16[8,128,128]{2,1,0:T(8,128)(2,1)} %bitcast.98), channel_id=1, source_target_pairs={{0,6},{2,8},{4,10},{6,12},{8,14},{10,16},{12,18},{14,20},{16,22},{... | collective-permute-start | bytes 786440 | tf_op jit(solution)/shard_map/ppermute | solution.py:12
  11.6 19.0 %collective-permute-start.2 = (bf16[8,128,128]{2,1,0:T(8,128)(2,1)}, bf16[8,128,128]{2,1,0:T(8,128)(2,1)S(1)}, u32[]{:S(2)}, u32[]{:S(2)}) collective-permute-start(bf16[8,128,128]{2,1,0:T(8,128)(2,1)} %bitcast.99), channel_id=1, source_target_pairs={{0,4},{2,6},{4,8},{6,10},{8,12},{10,14},{12,16},{14,18},{16,20},{1... | collective-permute-start | bytes 786440 | tf_op jit(solution)/shard_map/ppermute | solution.py:12
  12.8 25.4 %collective-permute-start.3 = (bf16[8,128,128]{2,1,0:T(8,128)(2,1)}, bf16[8,128,128]{2,1,0:T(8,128)(2,1)S(1)}, u32[]{:S(2)}, u32[]{:S(2)}) collective-permute-start(bf16[8,128,128]{2,1,0:T(8,128)(2,1)} %bitcast.100), channel_id=1, source_target_pairs={{0,2},{2,4},{4,6},{6,8},{8,10},{10,12},{12,14},{14,16},{16,18},{18... | collective-permute-start | bytes 786440 | tf_op jit(solution)/shard_map/ppermute | solution.py:12
  13.1 26.1 %collective-permute-start.4 = (bf16[8,128,128]{2,1,0:T(8,128)(2,1)}, bf16[8,128,128]{2,1,0:T(8,128)(2,1)S(1)}, u32[]{:S(2)}, u32[]{:S(2)}) collective-permute-start(bf16[8,128,128]{2,1,0:T(8,128)(2,1)} %bitcast.101), channel_id=1, source_target_pairs={{0,30},{2,0},{4,2},{6,4},{8,6},{10,8},{12,10},{14,12},{16,14},{18,... | collective-permute-start | bytes 786440 | tf_op jit(solution)/shard_map/ppermute | solution.py:12
  18.6 23.3 %copy-start.1 = (bf16[1024,128]{1,0:T(8,128)(2,1)S(1)}, bf16[1024,128]{1,0:T(8,128)(2,1)}, u32[]{:S(2)}) copy-start(bf16[1024,128]{1,0:T(8,128)(2,1)} %param.8) | copy-start | bytes 786436
  18.6 20.7 %collective-permute-start.5 = (bf16[8,128,128]{2,1,0:T(8,128)(2,1)}, bf16[8,128,128]{2,1,0:T(8,128)(2,1)S(1)}, u32[]{:S(2)}, u32[]{:S(2)}) collective-permute-start(bf16[8,128,128]{2,1,0:T(8,128)(2,1)} %bitcast.102), channel_id=1, source_target_pairs={{0,28},{2,30},{4,0},{6,2},{8,4},{10,6},{12,8},{14,10},{16,12},{18,... | collective-permute-start | bytes 786440 | tf_op jit(solution)/shard_map/ppermute | solution.py:12
  24.0 16.4 %collective-permute-start.6 = (bf16[8,128,128]{2,1,0:T(8,128)(2,1)}, bf16[8,128,128]{2,1,0:T(8,128)(2,1)S(1)}, u32[]{:S(2)}, u32[]{:S(2)}) collective-permute-start(bf16[8,128,128]{2,1,0:T(8,128)(2,1)} %bitcast.103), channel_id=1, source_target_pairs={{0,26},{2,28},{4,30},{6,0},{8,2},{10,4},{12,6},{14,8},{16,10},{18,... | collective-permute-start | bytes 786440 | tf_op jit(solution)/shard_map/ppermute | solution.py:12
  30.5 9.9 %collective-permute-start.7 = (bf16[8,128,128]{2,1,0:T(8,128)(2,1)}, bf16[8,128,128]{2,1,0:T(8,128)(2,1)S(1)}, u32[]{:S(2)}, u32[]{:S(2)}) collective-permute-start(bf16[8,128,128]{2,1,0:T(8,128)(2,1)} %bitcast.104), channel_id=1, source_target_pairs={{0,24},{2,26},{4,28},{6,30},{8,0},{10,2},{12,4},{14,6},{16,8},{18,... | collective-permute-start | bytes 786440 | tf_op jit(solution)/shard_map/ppermute | solution.py:12
  40.5 1.4 copy-start
  126.4 279.1 %copy-start.2 = (bf16[8,128,128]{2,1,0:T(8,128)(2,1)}, bf16[8,128,128]{2,1,0:T(8,128)(2,1)S(1)}, u32[]{:S(2)}) copy-start(bf16[8,128,128]{2,1,0:T(8,128)(2,1)S(1)} %get-tuple-element.45) | copy-start | bytes 786436
  127.3 251.4 %all-reduce.5.cloned.1.call-start = ((), (), s32[]{:S(2)}) async-start(), calls=%async_computation.1 | async-start | bytes 131072 | tf_op jit(solution)/shard_map/psum | solution.py:48
Sparse Core Ops, SparseCore 0:
  127.5 126.7 all-reduce.2
  260.4 118.3 all-reduce.4
where the time goes:
time: 414 us; the launch traced here: 412 us
  waiting for transfers between devices  263 us (64%)
  local copies, waits for them, and re-layouts  62.7 us (15%)
  other arithmetic  31.8 us (8%)
  matrix products  24.9 us (6%)
  starting transfers between devices  15.7 us (4%)
  between operations  14.2 us (3%)
    psum x1, waiting for transfers between devices, on_device(): lax.psum(jnp.dot(trial_full.T, sigma_full, precision=highest), ('blk', 'c...  127 us
    psum x1, waiting for transfers between devices, on_device(): lax.psum(jnp.dot(residual.T, residual, precision=highest), ('blk', 'col'))  120 us
    gather x8, local copies, waits for them, and re-layouts, one_block(): sources = stacked[chosen]  32.8 us
    gather x8, local copies, waits for them, and re-layouts, one_block(): coeffs = table[kinds]  20.7 us
    dot_general x8, matrix products, one_block(): jnp.einsum('jab,jbk->ak', coeffs, sources, preferred_element_type=jnp.flo...  19.6 us
    ppermute x8, starting transfers between devices, from_behind(): return lax.ppermute(value, axis, pairs)  15.7 us
    ppermute x8, waiting for transfers between devices, from_behind(): return lax.ppermute(value, axis, pairs)  15.6 us
    another operation x3, other arithmetic, on_device(): lower = jnp.linalg.cholesky(gram)  12.4 us
  transfers between devices with their start and end apart: 10, of which 6 were waited for; matrix products, arithmetic and copies ran while one was open for 1% of the time, Pallas kernels for 0%

commit v1 on v0

--- a/solution.py
+++ b/solution.py
@@ -45,7 +45,10 @@
         lax.psum(jnp.dot(trial_full.T, sigma_full, precision=highest), ("blk", "col")) / total
     )
     residual = sigma_full - jnp.dot(trial_full, projected, precision=highest)
-    gram = lax.psum(jnp.dot(residual.T, residual, precision=highest), ("blk", "col")) / total
+    gram = (
+        jnp.sum(lax.all_gather(jnp.dot(residual.T, residual, precision=highest), ("blk", "col")), 0)
+        / total
+    )
     lower = jnp.linalg.cholesky(gram)
     inverse = jax.scipy.linalg.solve_triangular(
         lower, jnp.eye(vec_count, dtype=jnp.float32), lower=True

time: 414 us -> 349 us (0.84)
  waiting for transfers between devices: 263 us -> 198 us
    psum x1 -> x0, waiting for transfers between devices: 120 us -> none  [on_device(): lax.psum(jnp.dot(residual.T, residual, precision=highest), ('blk', 'col'))]
    all_gather x0 -> x1, waiting for transfers between devices: none -> 55.3 us  [on_device(): lax.all_gather(jnp.dot(residual.T, residual, precision=highest), ('blk',...]
where the time goes in v1:
time: 349 us; the launch traced here: 347 us
  waiting for transfers between devices  198 us (57%)
  local copies, waits for them, and re-layouts  62.7 us (18%)
  other arithmetic  31.8 us (9%)
  matrix products  24.9 us (7%)
  starting transfers between devices  15.7 us (4%)
  between operations  14.2 us (4%)
    psum x1, waiting for transfers between devices, on_device(): lax.psum(jnp.dot(trial_full.T, sigma_full, precision=highest), ('blk', 'c...  127 us
    all_gather x1, waiting for transfers between devices, on_device(): lax.all_gather(jnp.dot(residual.T, residual, precision=highest), ('blk',...  55.3 us
    gather x8, local copies, waits for them, and re-layouts, one_block(): sources = stacked[chosen]  32.8 us
    gather x8, local copies, waits for them, and re-layouts, one_block(): coeffs = table[kinds]  20.7 us
    dot_general x8, matrix products, one_block(): jnp.einsum('jab,jbk->ak', coeffs, sources, preferred_element_type=jnp.flo...  19.6 us
    ppermute x8, starting transfers between devices, from_behind(): return lax.ppermute(value, axis, pairs)  15.7 us
    ppermute x8, waiting for transfers between devices, from_behind(): return lax.ppermute(value, axis, pairs)  15.6 us
    another operation x3, other arithmetic, on_device(): lower = jnp.linalg.cholesky(gram)  12.4 us
  transfers between devices with their start and end apart: 10, of which 6 were waited for; matrix products, arithmetic and copies ran while one was open for 1% of the time, Pallas kernels for 0%

profile of v1, /device:TPU:1, one launch (start us, length us, event | category | flops | bytes accessed | tf_op | source)
XLA Modules:
  0.0 347.1 jit_solution(7446727771374794062)
XLA Ops:
  7.2 2.2 collective-permute-start
  9.4 2.2 collective-permute-start.1
  11.6 1.2 collective-permute-start.2
  13.1 4.7 %collective-permute-start.4 = (bf16[8,128,128]{2,1,0:T(8,128)(2,1)}, bf16[8,128,128]{2,1,0:T(8,128)(2,1)S(1)}, u32[]{:S(2)}, u32[]{:S(2)}) collective-permute-start(bf16[8,128,128]{2,1,0:T(8,128)(2,1)} %bitcast.102), channel_id=1, source_target_pairs={{0,30},{2,0},{4,2},{6,4},{8,6},{10,8},{12,10},{14,12},{16,14},{18,... | collective-permute-start | bytes 786440 | tf_op jit(solution)/shard_map/ppermute | solution.py:12
  18.6 1.2 collective-permute-start.5
  19.8 4.2 %collective-permute-done.1 = bf16[8,128,128]{2,1,0:T(8,128)(2,1)S(1)} collective-permute-done((bf16[8,128,128]{2,1,0:T(8,128)(2,1)}, bf16[8,128,128]{2,1,0:T(8,128)(2,1)S(1)}, u32[]{:S(2)}, u32[]{:S(2)}) %collective-permute-start.1) | collective-permute-done | bytes 262176 | tf_op jit(solution)/shard_map/ppermute | solution.py:12
  24.0 2.3 collective-permute-start.6
  26.4 4.2 %collective-permute-done.2 = bf16[8,128,128]{2,1,0:T(8,128)(2,1)S(1)} collective-permute-done((bf16[8,128,128]{2,1,0:T(8,128)(2,1)}, bf16[8,128,128]{2,1,0:T(8,128)(2,1)S(1)}, u32[]{:S(2)}, u32[]{:S(2)}) %collective-permute-start.2) | collective-permute-done | bytes 262176 | tf_op jit(solution)/shard_map/ppermute | solution.py:12
  30.5 1.5 collective-permute-start.7
  32.1 6.1 %collective-permute-done.3 = bf16[8,128,128]{2,1,0:T(8,128)(2,1)S(1)} collective-permute-done((bf16[8,128,128]{2,1,0:T(8,128)(2,1)}, bf16[8,128,128]{2,1,0:T(8,128)(2,1)S(1)}, u32[]{:S(2)}, u32[]{:S(2)}) %collective-permute-start.3) | collective-permute-done | bytes 262176 | tf_op jit(solution)/shard_map/ppermute | solution.py:12
  38.2 1.0 constant_dynamic-update-slice_fusion
  39.3 1.0 collective-permute-done.6
  40.5 1.4 copy-done
  41.9 84.5 %while.10 = (s32[]{:T(128)}, bf16[8,128,128]{2,1,0:T(8,128)(2,1)S(1)}, s32[8,72]{1,0:T(8,128)}, bf16[64,128,128]{2,1,0:T(8,128)(2,1)}, s32[8,72]{1,0:T(8,128)S(1...) while((s32[]{:T(128)}, ...), condition=%wide.region_1.2_spmd, body=%wide.region_0.1_spmd.sunk | while | flops 302057920 | bytes 14233449 | solution.py:37
  42.6 2.6 gather_fusion
  45.2 4.1 %gather_fusion.1 = bf16[72,128,128]{2,1,0:T(8,128)(2,1)} fusion(bf16[72,128,128]{2,1,0:T(8,128)(2,1)} %get-tuple-element.146, s32[1024]{0:T(1024)S(1)} %pad_clamp_fusion.5), kind=kCustom, calls=%fused_computation.1.clone.1 | custom fusion | bytes 4718880 | tf_op jit(solution)/shard_map/while/body/eval_jaxpr/gather | solution.py:32
  50.0 2.4 fusion.34
  53.1 2.6 gather_fusion
  55.8 4.1 %gather_fusion.1 = bf16[72,128,128]{2,1,0:T(8,128)(2,1)} fusion(bf16[72,128,128]{2,1,0:T(8,128)(2,1)} %get-tuple-element.146, s32[1024]{0:T(1024)S(1)} %pad_clamp_fusion.5), kind=kCustom, calls=%fused_computation.1.clone.1 | custom fusion | bytes 4718880 | tf_op jit(solution)/shard_map/while/body/eval_jaxpr/gather | solution.py:32
  60.5 2.4 fusion.34
  63.7 2.6 gather_fusion
  66.3 4.1 %gather_fusion.1 = bf16[72,128,128]{2,1,0:T(8,128)(2,1)} fusion(bf16[72,128,128]{2,1,0:T(8,128)(2,1)} %get-tuple-element.146, s32[1024]{0:T(1024)S(1)} %pad_clamp_fusion.5), kind=kCustom, calls=%fused_computation.1.clone.1 | custom fusion | bytes 4718880 | tf_op jit(solution)/shard_map/while/body/eval_jaxpr/gather | solution.py:32
  71.1 2.4 fusion.34
  74.3 2.6 gather_fusion
  76.9 4.1 %gather_fusion.1 = bf16[72,128,128]{2,1,0:T(8,128)(2,1)} fusion(bf16[72,128,128]{2,1,0:T(8,128)(2,1)} %get-tuple-element.146, s32[1024]{0:T(1024)S(1)} %pad_clamp_fusion.5), kind=kCustom, calls=%fused_computation.1.clone.1 | custom fusion | bytes 4718880 | tf_op jit(solution)/shard_map/while/body/eval_jaxpr/gather | solution.py:32
  81.7 2.4 fusion.34
  84.8 2.6 gather_fusion
  87.5 4.1 %gather_fusion.1 = bf16[72,128,128]{2,1,0:T(8,128)(2,1)} fusion(bf16[72,128,128]{2,1,0:T(8,128)(2,1)} %get-tuple-element.146, s32[1024]{0:T(1024)S(1)} %pad_clamp_fusion.5), kind=kCustom, calls=%fused_computation.1.clone.1 | custom fusion | bytes 4718880 | tf_op jit(solution)/shard_map/while/body/eval_jaxpr/gather | solution.py:32
  92.2 2.4 fusion.34
  95.4 2.6 gather_fusion
  98.0 4.1 %gather_fusion.1 = bf16[72,128,128]{2,1,0:T(8,128)(2,1)} fusion(bf16[72,128,128]{2,1,0:T(8,128)(2,1)} %get-tuple-element.146, s32[1024]{0:T(1024)S(1)} %pad_clamp_fusion.5), kind=kCustom, calls=%fused_computation.1.clone.1 | custom fusion | bytes 4718880 | tf_op jit(solution)/shard_map/while/body/eval_jaxpr/gather | solution.py:32
  102.8 2.4 fusion.34
  106.0 2.6 gather_fusion
  108.6 4.1 %gather_fusion.1 = bf16[72,128,128]{2,1,0:T(8,128)(2,1)} fusion(bf16[72,128,128]{2,1,0:T(8,128)(2,1)} %get-tuple-element.146, s32[1024]{0:T(1024)S(1)} %pad_clamp_fusion.5), kind=kCustom, calls=%fused_computation.1.clone.1 | custom fusion | bytes 4718880 | tf_op jit(solution)/shard_map/while/body/eval_jaxpr/gather | solution.py:32
  113.4 2.4 fusion.34
  116.6 2.6 gather_fusion
  119.2 4.1 %gather_fusion.1 = bf16[72,128,128]{2,1,0:T(8,128)(2,1)} fusion(bf16[72,128,128]{2,1,0:T(8,128)(2,1)} %get-tuple-element.146, s32[1024]{0:T(1024)S(1)} %pad_clamp_fusion.5), kind=kCustom, calls=%fused_computation.1.clone.1 | custom fusion | bytes 4718880 | tf_op jit(solution)/shard_map/while/body/eval_jaxpr/gather | solution.py:32
  124.0 2.4 fusion.34
  126.4 0.9 convolution_bitcast_fusion.2
  127.5 126.7 %all-reduce.2.cloned.1.call-done = f32[128,128]{0,1:T(8,128)} async-done(((f32[128,128]{0,1:T(8,128)}), f32[128,128]{0,1:T(8,128)}) %all-reduce.2.cloned.1.call-update) | async-done | bytes 65552 | tf_op jit(solution)/shard_map/psum | solution.py:45
  254.2 1.2 fusion.9
  255.5 1.2 fusion.14
  256.7 0.8 broadcast_multiply_fusion
  258.3 55.3 %all-gather.3.cloned.1.call-done = f32[4096,128]{1,0:T(8,128)} async-done(((f32[128,128]{1,0:T(8,128)}), f32[4096,128]{1,0:T(8,128)}) %all-gather.3.cloned.1.call-update) | async-done | bytes 2097168 | tf_op jit(solution)/shard_map/all_gather | solution.py:49
  313.5 1.7 reduce_sum.11
  315.4 11.7 %cholesky.17 = f32[128,128]{1,0:T(8,128)S(1)} custom-call(f32[128,128]{1,0:T(8,128)S(1)} %fusion.13), custom_call_target="Cholesky" | custom-call | tf_op jit(solution)/shard_map/jit(cholesky)/cholesky | solution.py:52
  328.4 9.8 %custom-call.7 = f32[1,128,128]{1,2,0:T(8,128)S(1)} custom-call(f32[1,128,128]{2,1,0:T(8,128)S(1)} %fusion.10), custom_call_target="InvertDiagBlocksLowerTriangular" | custom-call | tf_op jit(solution)/shard_map/jit(_solve_triangular)/triangular_solve | solution.py:53
  338.5 1.8 fusion.15
  (64 shorter events, 15.2 us)
Async XLA Ops:
  7.2 247.1 %all-reduce.2.cloned.1.call-start = ((), (), s32[]{:S(2)}) async-start(), calls=%async_computation | async-start | bytes 131072 | tf_op jit(solution)/shard_map/psum | solution.py:45
  7.2 11.4 %collective-permute-start = (bf16[8,128,128]{2,1,0:T(8,128)(2,1)}, bf16[8,128,128]{2,1,0:T(8,128)(2,1)S(1)}, u32[]{:S(2)}, u32[]{:S(2)}) collective-permute-start(bf16[8,128,128]{2,1,0:T(8,128)(2,1)} %bitcast.98), channel_id=1, source_target_pairs={{0,8},{2,10},{4,12},{6,14},{8,16},{10,18},{12,20},{14,22},{16,24},... | collective-permute-start | bytes 786440 | tf_op jit(solution)/shard_map/ppermute | solution.py:12
  9.4 14.6 %collective-permute-start.1 = (bf16[8,128,128]{2,1,0:T(8,128)(2,1)}, bf16[8,128,128]{2,1,0:T(8,128)(2,1)S(1)}, u32[]{:S(2)}, u32[]{:S(2)}) collective-permute-start(bf16[8,128,128]{2,1,0:T(8,128)(2,1)} %bitcast.99), channel_id=1, source_target_pairs={{0,6},{2,8},{4,10},{6,12},{8,14},{10,16},{12,18},{14,20},{16,22},{... | collective-permute-start | bytes 786440 | tf_op jit(solution)/shard_map/ppermute | solution.py:12
  11.6 19.0 %collective-permute-start.2 = (bf16[8,128,128]{2,1,0:T(8,128)(2,1)}, bf16[8,128,128]{2,1,0:T(8,128)(2,1)S(1)}, u32[]{:S(2)}, u32[]{:S(2)}) collective-permute-start(bf16[8,128,128]{2,1,0:T(8,128)(2,1)} %bitcast.100), channel_id=1, source_target_pairs={{0,4},{2,6},{4,8},{6,10},{8,12},{10,14},{12,16},{14,18},{16,20},{1... | collective-permute-start | bytes 786440 | tf_op jit(solution)/shard_map/ppermute | solution.py:12
  12.8 25.4 %collective-permute-start.3 = (bf16[8,128,128]{2,1,0:T(8,128)(2,1)}, bf16[8,128,128]{2,1,0:T(8,128)(2,1)S(1)}, u32[]{:S(2)}, u32[]{:S(2)}) collective-permute-start(bf16[8,128,128]{2,1,0:T(8,128)(2,1)} %bitcast.101), channel_id=1, source_target_pairs={{0,2},{2,4},{4,6},{6,8},{8,10},{10,12},{12,14},{14,16},{16,18},{18... | collective-permute-start | bytes 786440 | tf_op jit(solution)/shard_map/ppermute | solution.py:12
  13.1 26.1 %collective-permute-start.4 = (bf16[8,128,128]{2,1,0:T(8,128)(2,1)}, bf16[8,128,128]{2,1,0:T(8,128)(2,1)S(1)}, u32[]{:S(2)}, u32[]{:S(2)}) collective-permute-start(bf16[8,128,128]{2,1,0:T(8,128)(2,1)} %bitcast.102), channel_id=1, source_target_pairs={{0,30},{2,0},{4,2},{6,4},{8,6},{10,8},{12,10},{14,12},{16,14},{18,... | collective-permute-start | bytes 786440 | tf_op jit(solution)/shard_map/ppermute | solution.py:12
  18.6 23.3 %copy-start.1 = (bf16[1024,128]{1,0:T(8,128)(2,1)S(1)}, bf16[1024,128]{1,0:T(8,128)(2,1)}, u32[]{:S(2)}) copy-start(bf16[1024,128]{1,0:T(8,128)(2,1)} %param.8) | copy-start | bytes 786436
  18.6 20.7 %collective-permute-start.5 = (bf16[8,128,128]{2,1,0:T(8,128)(2,1)}, bf16[8,128,128]{2,1,0:T(8,128)(2,1)S(1)}, u32[]{:S(2)}, u32[]{:S(2)}) collective-permute-start(bf16[8,128,128]{2,1,0:T(8,128)(2,1)} %bitcast.103), channel_id=1, source_target_pairs={{0,28},{2,30},{4,0},{6,2},{8,4},{10,6},{12,8},{14,10},{16,12},{18,... | collective-permute-start | bytes 786440 | tf_op jit(solution)/shard_map/ppermute | solution.py:12
  24.0 16.4 %collective-permute-start.6 = (bf16[8,128,128]{2,1,0:T(8,128)(2,1)}, bf16[8,128,128]{2,1,0:T(8,128)(2,1)S(1)}, u32[]{:S(2)}, u32[]{:S(2)}) collective-permute-start(bf16[8,128,128]{2,1,0:T(8,128)(2,1)} %bitcast.104), channel_id=1, source_target_pairs={{0,26},{2,28},{4,30},{6,0},{8,2},{10,4},{12,6},{14,8},{16,10},{18,... | collective-permute-start | bytes 786440 | tf_op jit(solution)/shard_map/ppermute | solution.py:12
  30.5 9.9 %collective-permute-start.7 = (bf16[8,128,128]{2,1,0:T(8,128)(2,1)}, bf16[8,128,128]{2,1,0:T(8,128)(2,1)S(1)}, u32[]{:S(2)}, u32[]{:S(2)}) collective-permute-start(bf16[8,128,128]{2,1,0:T(8,128)(2,1)} %bitcast.105), channel_id=1, source_target_pairs={{0,24},{2,26},{4,28},{6,30},{8,0},{10,2},{12,4},{14,6},{16,8},{18,... | collective-permute-start | bytes 786440 | tf_op jit(solution)/shard_map/ppermute | solution.py:12
  40.5 1.4 copy-start
  126.4 188.8 %copy-start.2 = (bf16[8,128,128]{2,1,0:T(8,128)(2,1)}, bf16[8,128,128]{2,1,0:T(8,128)(2,1)S(1)}, u32[]{:S(2)}) copy-start(bf16[8,128,128]{2,1,0:T(8,128)(2,1)S(1)} %get-tuple-element.45) | copy-start | bytes 786436
  127.3 186.2 %all-gather.3.cloned.1.call-start = ((), (), s32[]{:S(2)}) async-start(), calls=%async_computation.1 | async-start | bytes 2162688 | tf_op jit(solution)/shard_map/all_gather | solution.py:49
Sparse Core Ops, SparseCore 0:
  127.5 126.7 all-reduce.1
  257.7 55.8 all-gather.2
